TPU v7x, 256 devices: a whole 4x4x8 slice. The times are simulated.
256 devices in a mesh: sta: 64 (over z, x_lo, y), freq: 4 (over x_hi, core).
Axes of the slice: x: 4 (x_hi: 2, x_lo: 2; x = x_hi * 2 + x_lo), y: 4, z: 8, core: 2. Of those that a mesh axis runs over, the one named last changes fastest.
Arguments:
- spectra: bfloat16 [4, 2, 4096], P('freq', None, 'sta'), may hold values from -6 to 6
- green: bfloat16 [4, 2, 4096, 1024], P('freq', None, 'sta'), may hold values from -1.0546875 to 1.0546875
- source: float32 [4, 1024], P('freq'), may hold values from 0.25 to 4
- pair_mask: int32 [4096, 4096], P('sta'), may hold values 0 or 1
Outputs:
- new_source: float32 [4, 1024], P('freq')
- misfit: float32 [4], P('freq')
All inputs are finite; a program needn't handle non-finite values. No bound on the sum of `pair_mask` on one device may be relied on, other than what follows from the above.
Results may differ from a plain program's by a relative error of at most 0.0003.
Values may be sent and summed in bfloat16 or wider, within the bound.
No kernel may reach another device: no remote copies, remote signals or barrier semaphores. Data moves between devices by JAX's collectives and lax.ppermute only.
A program may use at most 64 MiB of HBM per device.

v0:
```python
import jax
import jax.numpy as jnp
from jax import lax
from jax.sharding import PartitionSpec as P


def copy_for_each(array, axis):
    peers = lax.axis_size(axis)
    return lax.all_to_all(
        jnp.broadcast_to(array[None], (peers, *array.shape)), axis, 0, 0, tiled=True
    )


def taken_together(array, axis):
    return copy_for_each(array, axis).sum(axis=0)


def in_one(arrays, axis):
    ends = [0]
    for a in arrays:
        ends.append(ends[-1] + a.size)
    total = taken_together(jnp.concatenate([a.ravel() for a in arrays]), axis)
    return tuple((total[b:e].reshape(a.shape) for a, b, e in zip(arrays, ends, ends[1:])))


def contract(a, b):
    return jnp.einsum("fix,fjx->fij", a, b, preferred_element_type=jnp.float32)


def spread(a, b):
    return jnp.einsum("fij,fjx->fix", a, b, preferred_element_type=jnp.float32)


def absorb(block_green, block_spec, weighted, spec_own, pair_mask):
    window = pair_mask.astype(jnp.float32)
    model_re = contract(weighted[:, 0], block_green[:, 0]) + contract(
        weighted[:, 1], block_green[:, 1]
    )
    model_im = contract(weighted[:, 1], block_green[:, 0]) - contract(
        weighted[:, 0], block_green[:, 1]
    )
    other = block_spec.astype(jnp.float32)
    data_re = (
        spec_own[:, 0, :, None] * other[:, 0, None, :]
        + spec_own[:, 1, :, None] * other[:, 1, None, :]
    )
    data_im = (
        spec_own[:, 1, :, None] * other[:, 0, None, :]
        - spec_own[:, 0, :, None] * other[:, 1, None, :]
    )
    resid_re = window[None] * (data_re - model_re)
    resid_im = window[None] * (data_im - model_im)
    mis = 0.5 * jnp.sum(resid_re * resid_re + resid_im * resid_im, axis=(1, 2))
    round_re = resid_re.astype(jnp.bfloat16)
    round_im = resid_im.astype(jnp.bfloat16)
    delta_re = spread(round_re, block_green[:, 0]) - spread(round_im, block_green[:, 1])
    delta_im = spread(round_re, block_green[:, 1]) + spread(round_im, block_green[:, 0])
    accum = jnp.stack([delta_re, delta_im], axis=1)
    return (accum, mis)


def local(spectra, green, source, pair_mask):
    count = lax.axis_size("sta")
    rows = green.shape[2]
    weighted = (source[:, None, None, :] * green).astype(jnp.bfloat16)
    spec_own = spectra.astype(jnp.float32)
    every_green, every_spec = (
        lax.all_gather(green, "sta", axis=2, tiled=True),
        lax.all_gather(spectra, "sta", axis=2, tiled=True),
    )
    state = absorb(every_green, every_spec, weighted, spec_own, pair_mask)
    accum, mis = state
    part = -jnp.sum(green * accum, axis=(1, 2))
    total_entries = green.shape[0] * lax.axis_size("freq") * green.shape[3]
    stations = rows * count
    grad, misfit = in_one((part, mis), "sta")
    squares = taken_together(jnp.sum(grad * grad), "freq")
    rms = jnp.sqrt(squares / total_entries + 1e-06)
    new_source = source * jnp.exp(-0.5 * grad / rms)
    return (new_source, misfit / (stations * stations))


def solution(mesh):
    placed = (P("freq", None, "sta"), P("freq", None, "sta", None), P("freq", None), P("sta", None))
    return jax.shard_map(
        local, mesh=mesh, in_specs=placed, out_specs=(P("freq", None), P("freq")), check_vma=False
    )
```

profile of v0, /device:TPU:1, one launch (start us, length us, event | category | flops | bytes accessed | tf_op | source)
XLA Modules:
  0.0 413.4 jit_solution(2978690009812199864)
XLA Ops:
  7.2 0.0 all-gather.2.cloned.1.call-start
  7.2 0.7 all-gather.2.cloned.1.call-update
  7.9 0.8 copy.9
  8.7 0.7 convert_element_type.26
  9.3 156.1 %all_gather.6 = bf16[1,2,4096]{1,0,2:T(2,128)(2,1)S(1)} all-gather(bf16[1,2,64]{1,0,2:T(2,128)(2,1)S(1)} %copy.9), channel_id=1, replica_groups=mesh['sta'=64,'freq'=4] {'sta'}, dimensions={2}, use_global_device_ids=true | all-gather | bytes 16640 | tf_op jit(solution)/shard_map/all_gather | solution.py:69
  165.4 2.2 convert_element_type.27
  167.6 1.0 fusion.18
  168.6 66.1 %slice_reduce_fusion.1 = (f32[4096]{0:T(1024)S(1)}, f32[4096]{0:T(1024)S(1)}) fusion(f32[1,2,4096]{1,0,2:T(1,128)S(1)} %convert_element_type.27), kind=kLoop, calls=%fused_computation.17 | loop fusion | bytes 65536 | tf_op jit(solution)/shard_map/slice | solution.py:44
  234.8 0.0 copy-start.2
  234.8 81.2 %all-gather.2.cloned.1.call-done = bf16[1,2,4096,1024]{3,2,1,0:T(8,128)(2,1)} async-done(((bf16[1,2,64,1024]{3,2,1,0:T(8,128)(2,1)}), bf16[1,2,4096,1024]{3,2,1,0:T(8,128)(2,1)}) %all-gather.2.cloned.1.call-update) | async-done | bytes 16777232 | tf_op jit(solution)/shard_map/all_gather | solution.py:68
  316.0 6.2 %fusion.3 = f32[64,4096]{1,0:T(8,128)S(1)} fusion(bf16[1,2,4096,1024]{3,2,1,0:T(8,128)(2,1)} %all-gather.2.cloned.1.call-done, bf16[1,2,64,1024]{3,2,1,0:T(8,128)(2,1)S(1)} %fusion.18), kind=kOutput, calls=%fused_computation.5 | convolution fusion | flops 536870912 | bytes 9568256 | tf_op jit(solution)/shard_map/fix,fjx->fij/dot_general | solution.py:27
  322.2 6.8 %fusion.1 = f32[64,4096]{1,0:T(8,128)S(1)} fusion(bf16[1,2,4096,1024]{3,2,1,0:T(8,128)(2,1)} %all-gather.2.cloned.1.call-done, bf16[1,2,64,1024]{3,2,1,0:T(8,128)(2,1)S(1)} %fusion.18), kind=kOutput, calls=%fused_computation.3 | convolution fusion | flops 536870912 | bytes 9568256 | tf_op jit(solution)/shard_map/fix,fjx->fij/dot_general | solution.py:27
  329.0 0.0 copy-done
  329.0 2.7 fusion.10
  331.7 1.6 fusion.2
  333.3 3.8 add_reduce_fusion
  337.0 1.6 fusion
  338.6 0.0 copy-start.1
  338.6 1.6 fusion.15
  340.2 0.0 copy-start.3
  340.2 1.6 fusion.17
  341.8 0.1 fusion.19
  342.6 0.2 broadcast_in_dim.4
  342.7 16.6 %all_to_all.12 = f32[64,1,1025]{2,1,0:T(1,128)S(1)} all-to-all(f32[64,1,1025]{2,1,0:T(1,128)S(1)} %broadcast_in_dim.4), channel_id=1, replica_groups=mesh['sta'=64,'freq'=4] {'sta'}, dimensions={0} | all-to-all | bytes 524800 | tf_op jit(solution)/shard_map/all_to_all | solution.py:9
  359.3 0.2 reduce_sum.47
  359.5 0.6 multiply_reduce_fusion
  360.1 0.6 slice.59
  360.7 1.2 broadcast_in_dim.5
  362.0 37.0 %all-to-all-start.1 = ((f32[4,1,1]{2,1,0:T(1,128)}), f32[4,1,1]{2,1,0:T(1,128)S(1)}, u32[]{:S(2)}, u32[]{:S(2)}) async-start(f32[4,1,1]{2,1,0:T(1,128)} %broadcast_in_dim.5), calls=%async_computation.1 | async-start | bytes 4096 | tf_op jit(solution)/shard_map/all_to_all | solution.py:9
  399.7 3.8 all-to-all-done.1
  403.5 0.6 reduce_sum.49
  404.8 0.6 mul.130
  (8 shorter events, 0.0 us)
Async XLA Ops:
  7.2 308.8 %all-gather.2.cloned.1.call-start = ((), (), s32[]{:S(2)}) async-start(), calls=%async_computation.2 | async-start | bytes 17039360 | tf_op jit(solution)/shard_map/all_gather | solution.py:68
  234.8 94.2 %copy-start.2 = (s32[64,4096]{1,0:T(8,128)S(1)}, s32[64,4096]{1,0:T(8,128)}, u32[]{:S(2)}) copy-start(s32[64,4096]{1,0:T(8,128)} %param.7) | copy-start | bytes 3145732
  316.0 13.0 %copy-start = (bf16[1,2,4096,1024]{3,2,1,0:T(8,128)(2,1)S(1)}, bf16[1,2,4096,1024]{3,2,1,0:T(8,128)(2,1)}, u32[]{:S(2)}) copy-start(bf16[1,2,4096,1024]{3,2,1,0:T(8,128)(2,1)} %all-gather.2.cloned.1.call-done) | copy-start | bytes 50331652
  338.6 3.2 copy-start.1
  340.2 64.6 %copy-start.3 = (f32[1,1024]{1,0:T(1,128)S(1)}, f32[1,1024]{1,0:T(1,128)}, u32[]{:S(2)}) copy-start(f32[1,1024]{1,0:T(1,128)} %param.6) | copy-start | bytes 12292
  362.0 41.5 %all-to-all-start.1 = ((f32[4,1,1]{2,1,0:T(1,128)}), f32[4,1,1]{2,1,0:T(1,128)S(1)}, u32[]{:S(2)}, u32[]{:S(2)}) async-start(f32[4,1,1]{2,1,0:T(1,128)} %broadcast_in_dim.5), calls=%async_computation.1 | async-start | bytes 4096 | tf_op jit(solution)/shard_map/all_to_all | solution.py:9
Sparse Core Ops, SparseCore 0:
  9.8 306.1 all-gather.1
where the time goes:
time: 414 us; the launch traced here: 413 us
  blocking collectives  173 us (42%)
  waiting for transfers between devices  85.7 us (21%)
  local copies, waits for them, and re-layouts  68.9 us (17%)
  starting transfers between devices  37.1 us (9%)
  matrix products  25.7 us (6%)
  between operations  17.4 us (4%)
  other arithmetic  5.96 us (1%)
    all_gather x1, blocking collectives, local(): lax.all_gather(spectra, 'sta', axis=2, tiled=True)  156 us
    all_gather x1, waiting for transfers between devices, local(): lax.all_gather(green, 'sta', axis=2, tiled=True)  81.2 us
    slice x1, local copies, waits for them, and re-layouts, absorb(): other[:, 0, None, :]  66.1 us
    all_to_all x1, starting transfers between devices, copy_for_each(): lax.all_to_all(jnp.broadcast_to(array[None], (peers, *array.shape)), axis...  37 us
    dot_general x4, matrix products, contract(): return jnp.einsum('fix,fjx->fij', a, b, preferred_element_type=jnp.float32)  19.4 us
    all_to_all x1, blocking collectives, copy_for_each(): lax.all_to_all(jnp.broadcast_to(array[None], (peers, *array.shape)), axis...  16.6 us
  transfers between devices with their start and end apart: 2, of which 2 were waited for; matrix products, arithmetic and copies ran while one was open for 17% of the time, Pallas kernels for 0%

commit v1 on v0

--- a/solution.py
+++ b/solution.py
@@ -64,8 +64,16 @@
     rows = green.shape[2]
     weighted = (source[:, None, None, :] * green).astype(jnp.bfloat16)
     spec_own = spectra.astype(jnp.float32)
+
+    def test_scenes(packet):
+        items = []
+        for _ in range(jax.lax.axis_size("sta")):
+            items.append(packet)
+        reply = jnp.concatenate(jax.lax.all_to_all(jnp.stack(items), "sta", 0, 0), axis=2)
+        return reply
+
     every_green, every_spec = (
-        lax.all_gather(green, "sta", axis=2, tiled=True),
+        test_scenes(green),
         lax.all_gather(spectra, "sta", axis=2, tiled=True),
     )
     state = absorb(every_green, every_spec, weighted, spec_own, pair_mask)

time: 414 us -> 682 us (1.65)
  blocking collectives: 173 us -> 521 us
  waiting for transfers between devices: 85.7 us -> 3.8 us
  local copies, waits for them, and re-layouts: 68.9 us -> 83.5 us
  between operations: 17.4 us -> 3.97 us
  starting transfers between devices: 37.1 us -> 46.7 us
  matrix products: 25.7 us -> 18 us
    all_gather x1, blocking collectives: 156 us -> 506 us  [local(): lax.all_gather(spectra, 'sta', axis=2, tiled=True)]
    all_gather x1 -> x0, waiting for transfers between devices: 81.2 us -> none  [local(): lax.all_gather(green, 'sta', axis=2, tiled=True)]
    all_to_all x0 -> x1, starting transfers between devices: none -> 14 us  [test_scenes(): jax.lax.all_to_all(jnp.stack(items), 'sta', 0, 0)]
    all_to_all x0 -> x1, local copies, waits for them, and re-layouts: none -> 8.76 us  [test_scenes(): jax.lax.all_to_all(jnp.stack(items), 'sta', 0, 0)]
    dot_general x4, matrix products: 19.4 us -> 11.8 us  [contract(): return jnp.einsum('fix,fjx->fij', a, b, preferred_element_type=jnp.float32)]
  transfers between devices with their start and end apart: 2 -> 2, of which waited for: 2 -> 1; matrix products, arithmetic and copies ran while one was open for 17% -> 10% of each run, Pallas kernels for 0% -> 0%
where the time goes in v1:
time: 682 us; the launch traced here: 681 us
  blocking collectives  521 us (76%)
  local copies, waits for them, and re-layouts  83.5 us (12%)
  starting transfers between devices  46.7 us (7%)
  matrix products  18 us (3%)
    all_gather x1, blocking collectives, local(): lax.all_gather(spectra, 'sta', axis=2, tiled=True)  506 us
    slice x1, local copies, waits for them, and re-layouts, absorb(): other[:, 0, None, :]  65.9 us
    all_to_all x1, starting transfers between devices, copy_for_each(): lax.all_to_all(jnp.broadcast_to(array[None], (peers, *array.shape)), axis...  32.7 us
    all_to_all x1, blocking collectives, copy_for_each(): lax.all_to_all(jnp.broadcast_to(array[None], (peers, *array.shape)), axis...  14.8 us
    all_to_all x1, starting transfers between devices, test_scenes(): jax.lax.all_to_all(jnp.stack(items), 'sta', 0, 0)  14 us
  transfers between devices with their start and end apart: 2, of which 1 were waited for; matrix products, arithmetic and copies ran while one was open for 10% of the time, Pallas kernels for 0%

profile of v1, /device:TPU:1, one launch (start us, length us, event | category | flops | bytes accessed | tf_op | source)
XLA Modules:
  0.0 681.2 jit_solution(8052288296891900131)
XLA Ops:
  0.6 6.7 stack.8
  7.3 14.0 %all-to-all-start = ((bf16[64,1,2,64,1024]{4,3,2,1,0:T(8,128)(2,1)}), bf16[64,1,2,64,1024]{4,3,2,1,0:T(8,128)(2,1)}, u32[]{:S(2)}, u32[]{:S(2)}) async-start(bf16[64,1,2,64,1024]{4,3,2,1,0:T(8,128)(2,1)} %stack.8), calls=%async_computation | async-start | bytes 33554432 | tf_op jit(solution)/shard_map/all_to_all | solution.py:72
  21.3 0.0 copy-done.3
  21.4 0.1 copy.12
  21.5 506.1 %all_gather.3 = bf16[1,2,4096]{1,0,2:T(2,128)(2,1)S(1)} all-gather(bf16[1,2,64]{1,0,2:T(2,128)(2,1)S(1)} %copy.12), channel_id=1, replica_groups=mesh['sta'=64,'freq'=4] {'sta'}, dimensions={2}, use_global_device_ids=true | all-gather | bytes 16640 | tf_op jit(solution)/shard_map/all_gather | solution.py:77
  527.6 2.2 convert_element_type.27
  529.8 0.0 copy-done
  529.8 0.0 copy-done.2
  529.8 65.9 %slice_reduce_fusion.1 = (f32[4096]{0:T(1024)S(1)}, f32[4096]{0:T(1024)S(1)}) fusion(f32[1,2,4096]{1,0,2:T(1,128)S(1)} %convert_element_type.27), kind=kLoop, calls=%fused_computation.17 | loop fusion | bytes 65536 | tf_op jit(solution)/shard_map/slice | solution.py:44
  595.8 0.0 all-to-all-done
  595.8 8.8 %copy.13 = bf16[64,1,2,64,1024]{4,3,0,2,1:T(8,128)(2,1)S(1)} copy(bf16[64,1,2,64,1024]{4,3,2,1,0:T(8,128)(2,1)} %all-to-all-done) | data formatting | bytes 33554432 | tf_op jit(solution)/shard_map/all_to_all | solution.py:72
  604.6 0.0 copy-start.1
  604.6 2.7 fusion.3
  607.2 2.7 fusion.1
  609.9 0.0 copy-done.1
  609.9 2.7 fusion.10
  612.6 1.6 fusion.2
  614.2 3.8 add_reduce_fusion
  617.9 1.6 fusion
  619.5 1.6 fusion.15
  621.1 1.6 fusion.17
  622.7 0.1 fusion.19
  623.4 0.2 broadcast_in_dim.4
  623.6 14.8 %all_to_all.17 = f32[64,1,1025]{2,1,0:T(1,128)S(1)} all-to-all(f32[64,1,1025]{2,1,0:T(1,128)S(1)} %broadcast_in_dim.4), channel_id=1, replica_groups=mesh['sta'=64,'freq'=4] {'sta'}, dimensions={0} | all-to-all | bytes 524800 | tf_op jit(solution)/shard_map/all_to_all | solution.py:9
  638.3 0.2 reduce_sum.47
  638.5 0.6 multiply_reduce_fusion
  639.1 0.6 slice.59
  639.7 1.2 broadcast_in_dim.5
  640.9 32.7 %all-to-all-start.2 = ((f32[4,1,1]{2,1,0:T(1,128)}), f32[4,1,1]{2,1,0:T(1,128)S(1)}, u32[]{:S(2)}, u32[]{:S(2)}) async-start(f32[4,1,1]{2,1,0:T(1,128)} %broadcast_in_dim.5), calls=%async_computation.2 | async-start | bytes 4096 | tf_op jit(solution)/shard_map/all_to_all | solution.py:9
  674.4 3.8 all-to-all-done.2
  678.2 0.6 reduce_sum.49
  679.5 0.6 mul.130
  (9 shorter events, 0.1 us)
Async XLA Ops:
  7.3 14.0 %copy-start.3 = (bf16[1,2,64]{2,1,0:T(2,128)(2,1)S(1)}, bf16[1,2,64]{2,1,0:T(2,128)(2,1)}, u32[]{:S(2)}) copy-start(bf16[1,2,64]{2,1,0:T(2,128)(2,1)} %param.4) | copy-start | bytes 772
  7.3 522.4 %copy-start = (bf16[1,2,64,1024]{3,2,1,0:T(8,128)(2,1)S(1)}, bf16[1,2,64,1024]{3,2,1,0:T(8,128)(2,1)}, u32[]{:S(2)}) copy-start(bf16[1,2,64,1024]{3,2,1,0:T(8,128)(2,1)} %param.5) | copy-start | bytes 786436
  7.3 522.4 %copy-start.2 = (f32[1,1024]{1,0:T(1,128)S(1)}, f32[1,1024]{1,0:T(1,128)}, u32[]{:S(2)}) copy-start(f32[1,1024]{1,0:T(1,128)} %param.6) | copy-start | bytes 12292
  7.3 588.4 %all-to-all-start = ((bf16[64,1,2,64,1024]{4,3,2,1,0:T(8,128)(2,1)}), bf16[64,1,2,64,1024]{4,3,2,1,0:T(8,128)(2,1)}, u32[]{:S(2)}, u32[]{:S(2)}) async-start(bf16[64,1,2,64,1024]{4,3,2,1,0:T(8,128)(2,1)} %stack.8), calls=%async_computation | async-start | bytes 33554432 | tf_op jit(solution)/shard_map/all_to_all | solution.py:72
  604.6 5.3 copy-start.1
  640.9 37.2 %all-to-all-start.2 = ((f32[4,1,1]{2,1,0:T(1,128)}), f32[4,1,1]{2,1,0:T(1,128)S(1)}, u32[]{:S(2)}, u32[]{:S(2)}) async-start(f32[4,1,1]{2,1,0:T(1,128)} %broadcast_in_dim.5), calls=%async_computation.2 | async-start | bytes 4096 | tf_op jit(solution)/shard_map/all_to_all | solution.py:9
